TPU v7x, 32 devices: a whole 2x2x4 slice. The times are simulated.
32 devices in a mesh: dp: 16 (over z, x, core), tp: 2 (over y).
Axes of the slice: x: 2, y: 2, z: 4, core: 2. Of those that a mesh axis runs over, the one named last changes fastest.
Arguments:
- tokens: bfloat16 [8192, 768], P('dp'), may hold values from -6 to 6
- neighbours: bfloat16 [128, 128, 768], P('dp'), may hold values from -6 to 6
- out_grad: bfloat16 [8192, 768], P('dp'), may hold values from -6 to 6
- group_sizes: int32 [16], P('dp'), may hold values from 1 to 4, as said below
- seq_lengths: int32 [16, 4], P('dp'), may hold values from 0 to 512, as said below
- stretch_neighbours: int32 [128, 2], P('dp'), may hold values from 0 to 7, as said below
- norm_gain: float32 [3, 768], replicated, may hold values from 0.5 to 1.5
- norm_bias: float32 [3, 768], replicated, may hold values from -1 to 1
- self_qkv_w: bfloat16 [768, 3, 768], P(None, None, 'tp'), may hold values from -0.3125 to 0.3125
- self_qkv_b: float32 [3, 768], P(None, 'tp'), may hold values from -1 to 1
- self_out_w: bfloat16 [768, 768], P('tp'), may hold values from -0.875 to 0.875
- self_out_b: float32 [768], replicated, may hold values from -1 to 1
- cross_q_w: bfloat16 [768, 768], P(None, 'tp'), may hold values from -0.3125 to 0.3125
- cross_q_b: float32 [768], P('tp'), may hold values from -1 to 1
- cross_kv_w: bfloat16 [768, 2, 768], P(None, None, 'tp'), may hold values from -0.3125 to 0.3125
- cross_v_b: float32 [768], P('tp'), may hold values from -1 to 1
- cross_out_w: bfloat16 [768, 768], P('tp'), may hold values from -0.875 to 0.875
- cross_out_b: float32 [768], replicated, may hold values from -1 to 1
- mlp_in_w: bfloat16 [768, 3072], P(None, 'tp'), may hold values from -0.21875 to 0.21875
- mlp_in_b: float32 [3072], P('tp'), may hold values from -1 to 1
- mlp_out_w: bfloat16 [3072, 768], P('tp'), may hold values from -0.21875 to 0.21875
- mlp_out_b: float32 [768], replicated, may hold values from -1 to 1
Outputs:
- output: bfloat16 [8192, 768], P('dp', 'tp')
- tokens_grad: bfloat16 [8192, 768], P('dp', 'tp')
- neighbours_grad: bfloat16 [128, 128, 768], P('dp', None, 'tp')
- norm_gain_grad: float32 [3, 768], replicated
- norm_bias_grad: float32 [3, 768], replicated
- self_qkv_w_grad: float32 [768, 3, 768], P('dp', None, 'tp')
- self_qkv_b_grad: float32 [3, 768], P(None, 'tp')
- self_out_w_grad: float32 [768, 768], P('tp', 'dp')
- self_out_b_grad: float32 [768], replicated
- cross_q_w_grad: float32 [768, 768], P('dp', 'tp')
- cross_q_b_grad: float32 [768], P('tp')
- cross_kv_w_grad: float32 [768, 2, 768], P('dp', None, 'tp')
- cross_v_b_grad: float32 [768], P('tp')
- cross_out_w_grad: float32 [768, 768], P('tp', 'dp')
- cross_out_b_grad: float32 [768], replicated
- mlp_in_w_grad: float32 [768, 3072], P('dp', 'tp')
- mlp_in_b_grad: float32 [3072], P('tp')
- mlp_out_w_grad: float32 [3072, 768], P('tp', 'dp')
- mlp_out_b_grad: float32 [768], replicated
Inputs may be any that keep to these rules, and one draw needn't show every extreme that they name: `group_sizes`: a power of two; bucket b's padded sequence length is 512 // group_sizes[b]; some device has 1 and some has 4 in every draw. `seq_lengths`: slots at or beyond the device's group size are 0; the others lie between a quarter of the padded length and the padded length; the first slot of every device is exactly its padded length. `stretch_neighbours`: indices into the owning device's own 8 stored neighbours; the two of a block differ.
All inputs are finite; a program needn't handle non-finite values.
Results may differ from a plain program's by a relative error of at most 0.024.
The roundings to bfloat16 on the way count: a program that leaves them out, or rounds other values in their place, can miss the bound.
Values sent between devices are 32-bit elements; how exact they have to be, the bound alone decides.
No kernel may reach another device: no remote copies, remote signals or barrier semaphores. Data moves between devices by JAX's collectives and lax.ppermute only.
A program may use at most 192 MiB of HBM per device.

v0:
```python
from functools import partial
import math
import jax
import jax.numpy as jnp
from jax import lax
from jax.sharding import PartitionSpec as P

HEAD_DIM = 64
STRETCH = 64


def norm_forward(field, gain, shift):
    center = field - jnp.mean(field, axis=-1, keepdims=True)
    spread = jnp.mean(center * center, axis=-1, keepdims=True)
    return center * lax.rsqrt(spread + 1e-05) * gain + shift


def norm_backward(field, gain, shift, gradient):
    result, pullback = jax.vjp(norm_forward, field, gain, shift)
    return pullback(gradient)


def exact_gelu(field):
    return jax.nn.gelu(field, approximate=False)


def rotate(field, position, direction):
    halfway = field.shape[-1] // 2
    frequency = jnp.exp(-math.log(10000.0) * jnp.arange(halfway, dtype=jnp.float32) / halfway)
    angles = position.astype(jnp.float32)[:, None] * frequency[None, :]
    cosine = jnp.cos(angles)[:, None, :]
    sine_part = jnp.sin(angles)[:, None, :] * direction
    first_half = field[..., :halfway]
    second_half = field[..., halfway:]
    return jnp.concatenate(
        [
            first_half * cosine - second_half * sine_part,
            second_half * cosine + first_half * sine_part,
        ],
        axis=-1,
    )


def head_scores(query, key_rows, allowed):
    raw_scores = (
        jnp.einsum("qd,kd->qk", query, key_rows, preferred_element_type=jnp.float32) * 0.125
    )
    return jnp.where(allowed, raw_scores, -1e30)


def head_forward(inputs, allowed):
    query, key_rows, value_rows = inputs
    scores = head_scores(query, key_rows, allowed)
    top_score = jnp.max(scores, axis=-1, keepdims=True)
    expo = jnp.exp(scores - top_score)
    total = jnp.sum(expo, axis=-1, keepdims=True)
    probs = (expo / total).astype(jnp.bfloat16)
    mixed = jnp.einsum("qk,kd->qd", probs, value_rows, preferred_element_type=jnp.float32)
    return (mixed, top_score + jnp.log(total))


def head_backward(inputs, allowed):
    query, key_rows, value_rows, row_lse, grad_mix = inputs
    weights = jnp.exp(head_scores(query, key_rows, allowed) - row_lse)
    grad_weights = jnp.einsum("qd,kd->qk", grad_mix, value_rows, preferred_element_type=jnp.float32)
    delta = jnp.sum(weights * grad_weights, axis=-1, keepdims=True)
    grad_scores = (weights * (grad_weights - delta)).astype(jnp.bfloat16)
    grad_query = (
        jnp.einsum("qk,kd->qd", grad_scores, key_rows, preferred_element_type=jnp.float32) * 0.125
    )
    grad_keys = (
        jnp.einsum("qk,qd->kd", grad_scores, query, preferred_element_type=jnp.float32) * 0.125
    )
    grad_values = jnp.einsum(
        "qk,qd->kd", weights.astype(jnp.bfloat16), grad_mix, preferred_element_type=jnp.float32
    )
    return (grad_query, grad_keys, grad_values)


def softmax_parts(scores):
    top_score = jnp.max(scores, axis=-1, keepdims=True)
    expo = jnp.exp(scores - top_score)
    total = jnp.sum(expo, axis=-1, keepdims=True)
    return (expo / total, top_score + jnp.log(total))


def per_device(
    tokens,
    neighbours,
    out_grad,
    group_sizes,
    seq_lengths,
    stretch_neighbours,
    norm_gain,
    norm_bias,
    self_qkv_w,
    self_qkv_b,
    self_out_w,
    self_out_b,
    cross_q_w,
    cross_q_b,
    cross_kv_w,
    cross_v_b,
    cross_out_w,
    cross_out_b,
    mlp_in_w,
    mlp_in_b,
    mlp_out_w,
    mlp_out_b,
):
    count = tokens.shape[0]
    width = tokens.shape[1]
    local = self_qkv_w.shape[2]
    heads = local // HEAD_DIM
    stretches = stretch_neighbours.shape[0]
    stored = neighbours.shape[0]
    span = neighbours.shape[1]
    padded = count // group_sizes[0]
    row_ids = jnp.arange(count, dtype=jnp.int32)
    position = row_ids % padded
    sequence = row_ids // padded
    slot_ids = jnp.arange(seq_lengths.shape[1], dtype=jnp.int32)
    tok_len = jnp.sum(
        jnp.where(sequence[:, None] == slot_ids[None, :], seq_lengths[0][None, :], 0), axis=1
    )
    allowed = (
        (sequence[:, None] == sequence[None, :])
        & (position[None, :] <= position[:, None])
        & (position[None, :] < tok_len[None, :])
    )
    shifted = position + (STRETCH - 1)
    valid = ((shifted < padded) & (shifted < tok_len)).astype(jnp.float32)[:, None]
    resid = tokens.astype(jnp.float32)
    own_width = width // lax.axis_size("tp")
    own_start = lax.axis_index("tp") * own_width
    ln_one = norm_forward(resid, norm_gain[0], norm_bias[0]).astype(jnp.bfloat16)
    qkv_pre = (
        jnp.einsum("td,dcf->tcf", ln_one, self_qkv_w, preferred_element_type=jnp.float32)
        + self_qkv_b
    )
    query = rotate(qkv_pre[:, 0].reshape(count, heads, HEAD_DIM), position, 1.0).astype(
        jnp.bfloat16
    )
    key_rows = rotate(qkv_pre[:, 1].reshape(count, heads, HEAD_DIM), position, 1.0).astype(
        jnp.bfloat16
    )
    value_rows = qkv_pre[:, 2].reshape(count, heads, HEAD_DIM).astype(jnp.bfloat16)
    head_query = jnp.swapaxes(query, 0, 1)
    head_keys = jnp.swapaxes(key_rows, 0, 1)
    head_values = jnp.swapaxes(value_rows, 0, 1)
    head_mix, self_lse = lax.map(
        partial(head_forward, allowed=allowed), (head_query, head_keys, head_values)
    )
    self_mix = jnp.swapaxes(head_mix, 0, 1).reshape(count, local).astype(jnp.bfloat16)
    attn = (
        lax.psum(jnp.dot(self_mix, self_out_w, preferred_element_type=jnp.float32), "tp")
        + self_out_b
    )
    hidden_one = resid + attn
    ln_two = norm_forward(hidden_one, norm_gain[1], norm_bias[1]).astype(jnp.bfloat16)
    cross_query = (
        jnp.dot(ln_two, cross_q_w, preferred_element_type=jnp.float32) + cross_q_b
    ).astype(jnp.bfloat16)
    flat_store = neighbours.reshape(stored * span, width)
    kv_bias = jnp.stack([jnp.zeros_like(cross_v_b), cross_v_b])
    store_kv = (
        jnp.einsum("nd,dcf->ncf", flat_store, cross_kv_w, preferred_element_type=jnp.float32)
        + kv_bias
    ).astype(jnp.bfloat16)
    block_kv = store_kv.reshape(stored, span, 2, heads, HEAD_DIM)[stretch_neighbours].reshape(
        stretches, 2 * span, 2, heads, HEAD_DIM
    )
    block_keys = block_kv[:, :, 0]
    block_values = block_kv[:, :, 1]
    query_rows = jnp.roll(cross_query, -(STRETCH - 1), axis=0).reshape(
        stretches, STRETCH, heads, HEAD_DIM
    )
    cross_scores = (
        jnp.einsum("cqhd,ckhd->chqk", query_rows, block_keys, preferred_element_type=jnp.float32)
        * 0.125
    )
    cross_weights, cross_lse = softmax_parts(cross_scores)
    cross_probs = cross_weights.astype(jnp.bfloat16)
    cross_rows = jnp.einsum(
        "chqk,ckhd->cqhd", cross_probs, block_values, preferred_element_type=jnp.float32
    ).reshape(count, local)
    cross_mix = jnp.roll(cross_rows * valid, STRETCH - 1, axis=0).astype(jnp.bfloat16)
    cross = (
        lax.psum(jnp.dot(cross_mix, cross_out_w, preferred_element_type=jnp.float32), "tp")
        + cross_out_b
    )
    hidden_two = hidden_one + cross
    ln_three = norm_forward(hidden_two, norm_gain[2], norm_bias[2]).astype(jnp.bfloat16)
    pre_act = jnp.dot(ln_three, mlp_in_w, preferred_element_type=jnp.float32) + mlp_in_b
    act, gelu_pull = jax.vjp(exact_gelu, pre_act)
    act_low = act.astype(jnp.bfloat16)
    mlp = (
        lax.psum(jnp.dot(act_low, mlp_out_w, preferred_element_type=jnp.float32), "tp") + mlp_out_b
    )
    output = lax.dynamic_slice_in_dim(hidden_two + mlp, own_start, own_width, 1).astype(
        jnp.bfloat16
    )
    grad_out = out_grad.astype(jnp.float32)
    mlp_out_b_grad = jnp.sum(grad_out, axis=0)
    mlp_out_w_grad = jnp.einsum("tf,td->fd", act_low, out_grad, preferred_element_type=jnp.float32)
    grad_act = jnp.einsum("td,fd->tf", out_grad, mlp_out_w, preferred_element_type=jnp.float32)
    grad_pre = gelu_pull(grad_act)[0].astype(jnp.bfloat16)
    mlp_in_b_grad = jnp.sum(grad_pre.astype(jnp.float32), axis=0)
    mlp_in_w_grad = jnp.einsum("td,tf->df", ln_three, grad_pre, preferred_element_type=jnp.float32)
    grad_ln_three = lax.psum(
        jnp.einsum("tf,df->td", grad_pre, mlp_in_w, preferred_element_type=jnp.float32), "tp"
    )
    grad_in_three, gain_three, shift_three = norm_backward(
        hidden_two, norm_gain[2], norm_bias[2], grad_ln_three
    )
    grad_two = grad_out + grad_in_three
    grad_cross = grad_two.astype(jnp.bfloat16)
    cross_out_b_grad = jnp.sum(grad_cross.astype(jnp.float32), axis=0)
    cross_out_w_grad = jnp.einsum(
        "tf,td->fd", cross_mix, grad_cross, preferred_element_type=jnp.float32
    )
    grad_cross_mix = jnp.einsum(
        "td,fd->tf", grad_cross, cross_out_w, preferred_element_type=jnp.float32
    ).astype(jnp.bfloat16)
    grad_rows = (
        jnp.roll(grad_cross_mix, -(STRETCH - 1), axis=0) * valid.astype(jnp.bfloat16)
    ).reshape(stretches, STRETCH, heads, HEAD_DIM)
    cross_again = jnp.exp(
        jnp.einsum("cqhd,ckhd->chqk", query_rows, block_keys, preferred_element_type=jnp.float32)
        * 0.125
        - cross_lse
    )
    grad_probs = jnp.einsum(
        "cqhd,ckhd->chqk", grad_rows, block_values, preferred_element_type=jnp.float32
    )
    delta = jnp.sum(cross_again * grad_probs, axis=-1, keepdims=True)
    cross_grad_scores = (cross_again * (grad_probs - delta)).astype(jnp.bfloat16)
    grad_query_rows = (
        jnp.einsum(
            "chqk,ckhd->cqhd", cross_grad_scores, block_keys, preferred_element_type=jnp.float32
        )
        * 0.125
    )
    grad_block_keys = (
        jnp.einsum(
            "chqk,cqhd->ckhd", cross_grad_scores, query_rows, preferred_element_type=jnp.float32
        )
        * 0.125
    )
    grad_block_values = jnp.einsum(
        "chqk,cqhd->ckhd", cross_probs, grad_rows, preferred_element_type=jnp.float32
    )
    grad_query = jnp.roll(grad_query_rows.reshape(count, local), STRETCH - 1, axis=0).astype(
        jnp.bfloat16
    )
    cross_q_b_grad = jnp.sum(grad_query.astype(jnp.float32), axis=0)
    cross_q_w_grad = jnp.einsum("td,tf->df", ln_two, grad_query, preferred_element_type=jnp.float32)
    grad_ln_two_part = jnp.einsum(
        "tf,df->td", grad_query, cross_q_w, preferred_element_type=jnp.float32
    )
    grad_block_kv = jnp.stack([grad_block_keys, grad_block_values], axis=2).reshape(
        stretches * 2, span * 2 * local
    )
    owners = (
        stretch_neighbours.reshape(-1)[None, :] == jnp.arange(stored, dtype=jnp.int32)[:, None]
    ).astype(jnp.float32)
    grad_store = (
        jnp.dot(owners, grad_block_kv, precision=lax.Precision.HIGHEST)
        .reshape(stored * span, 2, local)
        .astype(jnp.bfloat16)
    )
    cross_v_b_grad = jnp.sum(grad_store[:, 1].astype(jnp.float32), axis=0)
    cross_kv_w_grad = jnp.einsum(
        "nd,ncf->dcf", flat_store, grad_store, preferred_element_type=jnp.float32
    )
    store_part = jnp.einsum(
        "ncf,dcf->nd", grad_store, cross_kv_w, preferred_element_type=jnp.float32
    ).reshape(stored, span, width)
    neighbours_grad = lax.psum_scatter(store_part, "tp", scatter_dimension=2, tiled=True).astype(
        jnp.bfloat16
    )
    grad_ln_two = lax.psum(grad_ln_two_part, "tp")
    grad_in_two, gain_two, shift_two = norm_backward(
        hidden_one, norm_gain[1], norm_bias[1], grad_ln_two
    )
    grad_one = grad_two + grad_in_two
    grad_attn = grad_one.astype(jnp.bfloat16)
    self_out_b_grad = jnp.sum(grad_attn.astype(jnp.float32), axis=0)
    self_out_w_grad = jnp.einsum(
        "tf,td->fd", self_mix, grad_attn, preferred_element_type=jnp.float32
    )
    grad_self_mix = jnp.einsum(
        "td,fd->tf", grad_attn, self_out_w, preferred_element_type=jnp.float32
    ).astype(jnp.bfloat16)
    head_grad_mix = jnp.swapaxes(grad_self_mix.reshape(count, heads, HEAD_DIM), 0, 1)
    head_dq, head_dk, head_dv = lax.map(
        partial(head_backward, allowed=allowed),
        (head_query, head_keys, head_values, self_lse, head_grad_mix),
    )
    grad_q_rot = rotate(jnp.swapaxes(head_dq, 0, 1), position, -1.0).reshape(count, local)
    grad_k_rot = rotate(jnp.swapaxes(head_dk, 0, 1), position, -1.0).reshape(count, local)
    grad_v_rows = jnp.swapaxes(head_dv, 0, 1).reshape(count, local)
    grad_qkv = jnp.stack([grad_q_rot, grad_k_rot, grad_v_rows], axis=1).astype(jnp.bfloat16)
    self_qkv_b_grad = jnp.sum(grad_qkv.astype(jnp.float32), axis=0)
    self_qkv_w_grad = jnp.einsum(
        "td,tcf->dcf", ln_one, grad_qkv, preferred_element_type=jnp.float32
    )
    grad_ln_one = lax.psum(
        jnp.einsum("tcf,dcf->td", grad_qkv, self_qkv_w, preferred_element_type=jnp.float32), "tp"
    )
    grad_in_one, gain_one, shift_one = norm_backward(resid, norm_gain[0], norm_bias[0], grad_ln_one)
    tokens_grad = lax.dynamic_slice_in_dim(grad_one + grad_in_one, own_start, own_width, 1).astype(
        jnp.bfloat16
    )
    (
        self_qkv_w_grad,
        self_out_w_grad,
        cross_q_w_grad,
        cross_kv_w_grad,
        cross_out_w_grad,
        mlp_in_w_grad,
        mlp_out_w_grad,
    ) = (
        lax.psum_scatter(self_qkv_w_grad, "dp", scatter_dimension=0, tiled=True),
        lax.psum_scatter(self_out_w_grad, "dp", scatter_dimension=1, tiled=True),
        lax.psum_scatter(cross_q_w_grad, "dp", scatter_dimension=0, tiled=True),
        lax.psum_scatter(cross_kv_w_grad, "dp", scatter_dimension=0, tiled=True),
        lax.psum_scatter(cross_out_w_grad, "dp", scatter_dimension=1, tiled=True),
        lax.psum_scatter(mlp_in_w_grad, "dp", scatter_dimension=0, tiled=True),
        lax.psum_scatter(mlp_out_w_grad, "dp", scatter_dimension=1, tiled=True),
    )
    gain_grads = jnp.stack([gain_one, gain_two, gain_three])
    shift_grads = jnp.stack([shift_one, shift_two, shift_three])
    (
        norm_gain_grad,
        norm_bias_grad,
        self_qkv_b_grad,
        self_out_b_grad,
        cross_q_b_grad,
        cross_v_b_grad,
        cross_out_b_grad,
        mlp_in_b_grad,
        mlp_out_b_grad,
    ) = lax.psum(
        (
            gain_grads,
            shift_grads,
            self_qkv_b_grad,
            self_out_b_grad,
            cross_q_b_grad,
            cross_v_b_grad,
            cross_out_b_grad,
            mlp_in_b_grad,
            mlp_out_b_grad,
        ),
        "dp",
    )
    return (
        output,
        tokens_grad,
        neighbours_grad,
        norm_gain_grad,
        norm_bias_grad,
        self_qkv_w_grad,
        self_qkv_b_grad,
        self_out_w_grad,
        self_out_b_grad,
        cross_q_w_grad,
        cross_q_b_grad,
        cross_kv_w_grad,
        cross_v_b_grad,
        cross_out_w_grad,
        cross_out_b_grad,
        mlp_in_w_grad,
        mlp_in_b_grad,
        mlp_out_w_grad,
        mlp_out_b_grad,
    )


def solution(mesh):
    placed = (
        P("dp", None),
        P("dp", None, None),
        P("dp", None),
        P("dp"),
        P("dp", None),
        P("dp", None),
        P(),
        P(),
        P(None, None, "tp"),
        P(None, "tp"),
        P("tp", None),
        P(),
        P(None, "tp"),
        P("tp"),
        P(None, None, "tp"),
        P("tp"),
        P("tp", None),
        P(),
        P(None, "tp"),
        P("tp"),
        P("tp", None),
        P(),
    )
    return jax.shard_map(
        per_device,
        mesh=mesh,
        in_specs=placed,
        out_specs=(
            P("dp", "tp"),
            P("dp", "tp"),
            P("dp", None, "tp"),
            P(),
            P(),
            P("dp", None, "tp"),
            P(None, "tp"),
            P("tp", "dp"),
            P(),
            P("dp", "tp"),
            P("tp"),
            P("dp", None, "tp"),
            P("tp"),
            P("tp", "dp"),
            P(),
            P("dp", "tp"),
            P("tp"),
            P("tp", "dp"),
            P(),
        ),
        check_vma=False,
    )
```

profile of v0, /device:TPU:0, one launch (start us, length us, event | category | flops | bytes accessed | tf_op | source)
XLA Modules:
  0.0 986.2 jit_solution(2578824090523314707)
XLA Ops:
  11.8 2.8 convolution_add_fusion.1
  20.6 2.4 subtract_convert_fusion.2
  24.2 2.2 copy.158
  28.2 2.2 copy.159
  30.4 20.7 %while.30 = (s32[]{:T(128)}, bf16[6,512,64]{1,2,0:T(8,128)(2,1)S(1)}, f32[6,512,1]{1,2,0:T(1,128)}, bf16[6,512,64]{2,1,0:T(8,128)(2,1)}, bf16[6,512,64]{2,1,0:T(...) while((s32[]{:T(128)}, ...), condition=%wide.region_6.7_spmd.clone.clone, body=%wide.region_3.6_spmd.clone.sunk.clone | while | flops 70254080 | bytes 3701353 | solution.py:151
  51.1 3.1 fusion.123
  55.1 4.3 add_convert_fusion.1
  59.4 2.7 copy.162
  62.2 2.0 copy.197
  65.8 4.0 gather_fusion
  69.8 6.0 copy.165
  75.8 5.6 reshape.384
  81.5 3.8 fusion.120
  85.3 23.3 %all-reduce.11.cloned.1.call-done = f32[512,768]{1,0:T(8,128)} async-done(((f32[512,768]{1,0:T(8,128)}), f32[512,768]{1,0:T(8,128)}) %all-reduce.11.cloned.1.call-update) | async-done | bytes 1572880 | tf_op jit(solution)/shard_map/psum | solution.py:156
  114.5 2.3 copy.181
  116.8 2.8 multiply_reduce_fusion.2
  122.2 2.4 convolution_bitcast_fusion.6
  124.6 2.1 copy.170
  126.6 2.6 reshape.386
  131.3 2.0 fusion.82
  134.4 50.7 %all-reduce.13.cloned.1.call-done = f32[512,768]{1,0:T(8,128)} async-done(((f32[512,768]{1,0:T(8,128)}), f32[512,768]{1,0:T(8,128)}) %all-reduce.13.cloned.1.call-update) | async-done | bytes 1572880 | tf_op jit(solution)/shard_map/psum | solution.py:189
  185.0 2.3 fusion.117
  190.1 10.2 %convert_reduce_fusion = (f32[1536]{0:T(1024)}, bf16[512,1536]{1,0:T(8,128)(2,1)S(1)}, f32[512,1536]{1,0:T(8,128)}) fusion(f32[512,1536]{1,0:T(8,128)S(1)} %convolution_add_fusion, bf16[512,768]{1,0:T(8,128)(2,1)S(1)} %copy-done.17, bf16[1536,768]{1,0:T(8,128)(2,1)S(1)} %copy-done), kind=kOutput, calls=%fused_computation.61 | convolution fusion | flops 1266153984 | bytes 11016192 | tf_op jit(solution)/shard_map/td,fd->tf/dot_general | solution.py:206
  201.5 2.6 fusion.125
  205.5 3.6 multiply_convert_fusion.2
  210.2 2.5 fusion.124
  212.7 43.0 %all-reduce.15.cloned.1.call-done = f32[512,768]{1,0:T(8,128)} async-done(((f32[512,768]{1,0:T(8,128)}), f32[512,768]{1,0:T(8,128)}) %all-reduce.15.cloned.1.call-update) | async-done | bytes 1572880 | tf_op jit(solution)/shard_map/psum | solution.py:210
  255.8 3.2 multiply_reduce_fusion.3
  264.7 3.7 multiply_reduce_fusion.1
  271.0 2.2 multiply_bitcast_fusion
  277.3 3.8 convolution_bitcast_fusion.2
  281.1 3.4 pad_maximum_fusion
  284.5 13.7 %copy.183 = f32[8,256,2,6,64]{4,3,2,1,0:T(8,128)} copy(f32[8,256,2,6,64]{1,4,3,0,2:T(8,128)} %pad_maximum_fusion) | data formatting | bytes 12582912 | tf_op jit(solution)/shard_map/stack | solution.py:261
  298.1 14.9 %reshape.389 = f32[16,98304]{1,0:T(8,128)} reshape(f32[8,256,2,6,64]{4,3,2,1,0:T(8,128)} %copy.183) | data formatting | bytes 12582912 | tf_op jit(solution)/shard_map/reshape | solution.py:261
  313.1 6.3 convolution_convert_fusion
  319.4 2.7 convert_element_type.173
  322.1 4.9 convolution_bitcast_fusion.4
  327.0 5.3 copy.188
  333.7 2.7 multiply_reduce_fusion.4
  341.5 57.1 %while.31 = (s32[]{:T(128)}, f32[6,512,64]{1,2,0:T(8,128)}, f32[6,512,64]{1,2,0:T(8,128)}, bf16[6,512,64]{1,2,0:T(8,128)(2,1)}, bf16[6,512,64]{2,1,0:T(8,128)(2,...) while((s32[]{:T(128)}, f32[6,512,64]{1,2,0:T(8,128)}, ...), condition=%wide.region_25.26_spmd.clone.clone, body=%wide.region_23.25_spmd.clone.sunk.clone | while | flops 171245056 | bytes 12345017 | solution.py:296
  347.3 2.0 fusion.206
  356.8 2.0 fusion.206
  366.3 2.0 fusion.206
  375.8 2.0 fusion.206
  385.4 2.0 fusion.206
  394.9 2.0 fusion.206
  402.2 4.0 convolution_bitcast_fusion.5
  407.7 4.5 convolution_bitcast_fusion.3
  417.1 3.2 fusion.108
  420.4 5.2 fusion.111
  426.7 5.0 fusion.126
  432.7 4.4 fusion.78
  439.5 3.6 fusion.62
  445.9 72.7 %all-reduce.21.cloned.1.call-done = (f32[512,768]{1,0:T(8,128)}, f32[512,768]{1,0:T(8,128)}) async-done(((f32[512,768]{1,0:T(8,128)}, f32[512,768]{1,0:T(8,128)}), (f32[512,768]{1,0:T(8,128)}, f32[512,768]{1,0:T(8,128)})) %all-reduce.21.cloned.1.call-update) | async-done | bytes 3145744 | tf_op jit(solution)/shard_map/psum | solution.py:198
  518.6 2.1 fusion.59
  520.8 61.8 %all-reduce.2 = (f32[3,768]{1,0:T(4,128)}, f32[3,768]{1,0:T(4,128)}, f32[3,384]{1,0:T(4,128)}, f32[768]{0:T(1024)}, f32[384]{0:T(512)}, /*index=5*/f32[384]{0:T(...) all-reduce(f32[3,768]{1,0:T(4,128)S(1)} %pad_maximum_fusion.12, ...), channel_id=1, replica_groups=mesh['dp'=16,'tp'=2] {'dp'}, use_global_device_ids=true, to_apply=%region_33.34 | all-reduce | flops 10368 | bytes 82944 | tf_op jit(solution)/shard_map/psum | solution.py:344
  582.6 2.2 fusion.114
  587.3 2.4 convert_element_type.169
  589.7 37.0 %reduce-scatter.16.cloned.1.call-done = f32[384,48]{0,1:T(8,128)} async-done(((f32[384,768]{0,1:T(8,128)}), f32[384,48]{0,1:T(8,128)}) %reduce-scatter.16.cloned.1.call-update) | async-done | bytes 73744 | tf_op jit(solution)/shard_map/reduce_scatter | solution.py:328
  626.7 61.4 %reduce-scatter.14.cloned.1.call-done = f32[48,384]{1,0:T(8,128)} async-done(((f32[768,384]{1,0:T(8,128)}), f32[48,384]{1,0:T(8,128)}) %reduce-scatter.14.cloned.1.call-update) | async-done | bytes 73744 | tf_op jit(solution)/shard_map/reduce_scatter | solution.py:326
  688.2 61.3 %reduce-scatter.12.cloned.1.call-done = f32[384,48]{0,1:T(8,128)} async-done(((f32[384,768]{0,1:T(8,128)}), f32[384,48]{0,1:T(8,128)}) %reduce-scatter.12.cloned.1.call-update) | async-done | bytes 73744 | tf_op jit(solution)/shard_map/reduce_scatter | solution.py:325
  749.4 79.0 %reduce-scatter.18.cloned.1.call-done = f32[48,1536]{1,0:T(8,128)} async-done(((f32[768,1536]{1,0:T(8,128)}), f32[48,1536]{1,0:T(8,128)}) %reduce-scatter.18.cloned.1.call-update) | async-done | bytes 294928 | tf_op jit(solution)/shard_map/reduce_scatter | solution.py:329
  828.5 79.1 %reduce-scatter.20.cloned.1.call-done = f32[1536,48]{0,1:T(8,128)} async-done(((f32[1536,768]{0,1:T(8,128)}), f32[1536,48]{0,1:T(8,128)}) %reduce-scatter.20.cloned.1.call-update) | async-done | bytes 294928 | tf_op jit(solution)/shard_map/reduce_scatter | solution.py:330
  907.5 71.9 %reduce-scatter.10.cloned.1.call-done = f32[48,3,384]{2,0,1:T(8,128)} async-done(((f32[768,3,384]{2,0,1:T(8,128)}), f32[48,3,384]{2,0,1:T(8,128)}) %reduce-scatter.10.cloned.1.call-update) | async-done | bytes 221200 | tf_op jit(solution)/shard_map/reduce_scatter | solution.py:324
  (436 shorter events, 135.9 us)
Async XLA Ops:
  7.2 182.9 %copy-start = (bf16[1536,768]{1,0:T(8,128)(2,1)S(1)}, bf16[1536,768]{1,0:T(8,128)(2,1)}, u32[]{:S(2)}) copy-start(bf16[1536,768]{1,0:T(8,128)(2,1)} %param.46) | copy-start | bytes 7077892
  7.2 3.0 copy-start.9
  7.2 101.4 %all-reduce.11.cloned.1.call-start = ((), (), s32[]{:S(2)}) async-start(), calls=%async_computation.7 | async-start | bytes 3145728 | tf_op jit(solution)/shard_map/psum | solution.py:156
  8.6 3.1 copy-start.108
  8.7 10.3 %copy-start.29 = (bf16[6,512,64]{1,2,0:T(8,128)(2,1)}, bf16[6,512,64]{1,2,0:T(8,128)(2,1)S(1)}, u32[]{:S(2)}) copy-start(bf16[6,512,64]{1,2,0:T(8,128)(2,1)S(1)} %fusion.122) | copy-start | bytes 1179652
  10.2 4.5 copy-start.68
  11.1 3.5 copy-start.74
  11.8 2.9 copy-start.66
  11.8 2.9 copy-start.97
  24.2 6.2 copy-start.34
  24.2 6.2 copy-start.90
  51.1 3.1 copy-start.32
  51.1 3.8 copy-start.95
  54.2 130.8 %all-reduce.13.cloned.1.call-start = ((), (), s32[]{:S(2)}) async-start(), calls=%async_computation.8 | async-start | bytes 3145728 | tf_op jit(solution)/shard_map/psum | solution.py:189
  81.5 27.2 %copy-start.101 = (f32[768]{0:T(1024)S(1)}, f32[768]{0:T(1024)}, u32[]{:S(2)}) copy-start(f32[768]{0:T(1024)} %param.37) | copy-start | bytes 9220
  119.6 85.2 %copy-start.60 = (f32[8,6,64]{2,1,0:T(8,128)}, f32[8,6,64]{2,1,0:T(8,128)S(1)}, u32[]{:S(2)}) copy-start(f32[8,6,64]{2,1,0:T(8,128)S(1)} %get-tuple-element.443) | copy-start | bytes 36868
  120.7 84.1 %copy-start.64 = (f32[8,6,64]{2,1,0:T(8,128)}, f32[8,6,64]{2,1,0:T(8,128)S(1)}, u32[]{:S(2)}) copy-start(f32[8,6,64]{2,1,0:T(8,128)S(1)} %fusion.50) | copy-start | bytes 36868
  126.6 2.6 copy-start.87
  131.3 53.7 %copy-start.94 = (f32[768]{0:T(1024)S(1)}, f32[768]{0:T(1024)}, u32[]{:S(2)}) copy-start(f32[768]{0:T(1024)} %param.43) | copy-start | bytes 9220
  133.3 122.4 %all-reduce.15.cloned.1.call-start = ((), (), s32[]{:S(2)}) async-start(), calls=%async_computation.9 | async-start | bytes 3145728 | tf_op jit(solution)/shard_map/psum | solution.py:210
  185.0 3.5 copy-start.106
  187.7 71.3 %copy-start.76 = (f32[512]{0:T(512)}, f32[512]{0:T(512)S(1)}, u32[]{:S(2)}) copy-start(f32[512]{0:T(512)S(1)} %fusion.101) | copy-start | bytes 6148
  190.1 10.2 %copy-start.37 = (f32[512,1536]{1,0:T(8,128)}, f32[512,1536]{1,0:T(8,128)S(1)}, u32[]{:S(2)}) copy-start(f32[512,1536]{1,0:T(8,128)S(1)} %convolution_add_fusion) | copy-start | bytes 9437188
  204.1 128.5 %all-reduce.17.cloned.1.call-start = ((), (), s32[]{:S(2)}) async-start(), calls=%async_computation.10 | async-start | bytes 3145728 | tf_op jit(solution)/shard_map/psum | solution.py:282
  212.7 46.2 %copy-start.7 = (f32[512,768]{1,0:T(8,128)S(1)}, f32[512,768]{1,0:T(8,128)}, u32[]{:S(2)}) copy-start(f32[512,768]{1,0:T(8,128)} %copy-done.6) | copy-start | bytes 4718596
  255.8 3.2 copy-start.23
  264.7 3.7 copy-start.35
  264.7 3.7 copy-start.5
  276.8 166.3 %all-reduce.19.cloned.1.call-start = ((), (), s32[]{:S(2)}) async-start(), calls=%async_computation.18 | async-start | bytes 4718592
  277.3 3.8 copy-start.14
  298.1 14.9 %copy-start.102 = (s32[16]{0:T(128)S(1)}, s32[16]{0:T(128)}, u32[]{:S(2)}) copy-start(s32[16]{0:T(128)} %eq.52) | copy-start | bytes 196
  322.1 4.9 copy-start.20
  332.4 186.2 %all-reduce.21.cloned.1.call-start = ((), (), s32[]{:S(2)}) async-start(), calls=%async_computation.19 | async-start | bytes 6291456 | tf_op jit(solution)/shard_map/psum | solution.py:198
  333.7 3.4 copy-start.22
  341.5 58.4 %copy-start.54 = (f32[512,32]{0,1:T(8,128)S(1)}, f32[512,32]{0,1:T(8,128)}, u32[]{:S(2)}) copy-start(f32[512,32]{0,1:T(8,128)} %copy-done.53) | copy-start | bytes 196612
  341.5 58.4 %copy-start.63 = (f32[512,32]{0,1:T(8,128)S(1)}, f32[512,32]{0,1:T(8,128)}, u32[]{:S(2)}) copy-start(f32[512,32]{0,1:T(8,128)} %get-tuple-element.438) | copy-start | bytes 196612
  347.3 3.8 copy-start.31
  356.8 3.8 copy-start.31
  366.3 3.8 copy-start.31
  375.8 3.8 copy-start.31
  385.3 3.8 copy-start.31
  394.9 3.8 copy-start.31
  401.9 4.3 copy-start.48
  402.2 4.1 copy-start.50
  406.2 181.1 %reduce-scatter.8.cloned.1.call-start = ((), (), s32[]{:S(2)}) async-start(), calls=%async_computation.11 | async-start | bytes 4718592 | tf_op jit(solution)/shard_map/reduce_scatter | solution.py:279
  412.2 3.0 copy-start.39
  412.2 3.0 copy-start.44
  412.2 214.5 %reduce-scatter.16.cloned.1.call-start = ((), (), s32[]{:S(2)}) async-start(), calls=%async_computation.15 | async-start | bytes 1253376 | tf_op jit(solution)/shard_map/reduce_scatter | solution.py:328
  415.1 273.0 %reduce-scatter.14.cloned.1.call-start = ((), (), s32[]{:S(2)}) async-start(), calls=%async_computation.14 | async-start | bytes 1253376 | tf_op jit(solution)/shard_map/reduce_scatter | solution.py:326
  417.0 3.4 copy-start.8
  417.0 3.4 copy-start.77
  417.0 3.4 copy-start.100
  417.0 332.4 %reduce-scatter.12.cloned.1.call-start = ((), (), s32[]{:S(2)}) async-start(), calls=%async_computation.13 | async-start | bytes 1253376 | tf_op jit(solution)/shard_map/reduce_scatter | solution.py:325
  420.3 408.2 %reduce-scatter.18.cloned.1.call-start = ((), (), s32[]{:S(2)}) async-start(), calls=%async_computation.16 | async-start | bytes 5013504 | tf_op jit(solution)/shard_map/reduce_scatter | solution.py:329
  425.6 482.0 %reduce-scatter.20.cloned.1.call-start = ((), (), s32[]{:S(2)}) async-start(), calls=%async_computation.17 | async-start | bytes 5013504 | tf_op jit(solution)/shard_map/reduce_scatter | solution.py:330
  431.8 547.7 %reduce-scatter.10.cloned.1.call-start = ((), (), s32[]{:S(2)}) async-start(), calls=%async_computation.12 | async-start | bytes 3760128 | tf_op jit(solution)/shard_map/reduce_scatter | solution.py:324
  437.1 7.5 copy-start.85
  437.2 7.5 copy-start.84
  439.5 5.2 copy-start.49
  444.7 76.1 %copy-start.80 = (f32[768]{0:T(1024)S(1)}, f32[768]{0:T(1024)}, u32[]{:S(2)}) copy-start(f32[768]{0:T(1024)} %get-tuple-element.401) | copy-start | bytes 9220
  444.7 76.1 %copy-start.81 = (f32[768]{0:T(1024)S(1)}, f32[768]{0:T(1024)}, u32[]{:S(2)}) copy-start(f32[768]{0:T(1024)} %get-tuple-element.431) | copy-start | bytes 9220
  444.7 76.1 %copy-start.88 = (f32[1536]{0:T(1024)S(1)}, f32[1536]{0:T(1024)}, u32[]{:S(2)}) copy-start(f32[1536]{0:T(1024)} %get-tuple-element.398) | copy-start | bytes 18436
  444.7 137.8 %copy-start.72 = (f32[512]{0:T(512)S(1)}, f32[512]{0:T(512)}, u32[]{:S(2)}) copy-start(f32[512]{0:T(512)} %copy-done.71) | copy-start | bytes 6148
  586.4 393.0 %copy-start.1 = (bf16[1536,768]{1,0:T(8,128)(2,1)S(1)}, bf16[1536,768]{1,0:T(8,128)(2,1)}, u32[]{:S(2)}) copy-start(bf16[1536,768]{1,0:T(8,128)(2,1)} %param.46) | copy-start | bytes 7077892
  (71 other events, 104.5 us)
Sparse Core Ops, SparseCore 0:
  54.3 54.2 all-reduce.10
  133.5 51.5 all-reduce.12
  204.2 51.5 all-reduce.14
  276.9 51.5 all-reduce.16
  332.5 98.9 all-reduce.18
  433.7 84.8 all-reduce.20
  520.8 43.4 reduce-scatter.7
  568.5 58.1 reduce-scatter.15
  630.9 57.1 reduce-scatter.13
  692.2 57.1 reduce-scatter.11
  753.9 74.5 reduce-scatter.17
  832.7 74.7 reduce-scatter.19
  912.0 67.3 reduce-scatter.9
where the time goes:
time: 995 us; the launch traced here: 986 us
  waiting for transfers between devices  580 us (58%)
  matrix products  152 us (15%)
  local copies, waits for them, and re-layouts  117 us (12%)
  blocking collectives  61.8 us (6%)
  other arithmetic  57.1 us (6%)
  between operations  16.9 us (2%)
    reduce_scatter x1, waiting for transfers between devices, per_device(): lax.psum_scatter(mlp_out_w_grad, 'dp', scatter_dimension=1, tiled=True)  79.1 us
    reduce_scatter x1, waiting for transfers between devices, per_device(): lax.psum_scatter(mlp_in_w_grad, 'dp', scatter_dimension=0, tiled=True)  79 us
    psum x1, waiting for transfers between devices, per_device(): lax.psum(jnp.dot(act_low, mlp_out_w, preferred_element_type=jnp.float32),...  72.7 us
    reduce_scatter x1, waiting for transfers between devices, per_device(): lax.psum_scatter(self_qkv_w_grad, 'dp', scatter_dimension=0, tiled=True)  71.9 us
    psum x1, blocking collectives, per_device(): lax.psum((gain_grads, shift_grads, self_qkv_b_grad, self_out_b_grad, cros...  61.8 us
    reduce_scatter x1, waiting for transfers between devices, per_device(): lax.psum_scatter(cross_q_w_grad, 'dp', scatter_dimension=0, tiled=True)  61.4 us
    reduce_scatter x1, waiting for transfers between devices, per_device(): lax.psum_scatter(self_out_w_grad, 'dp', scatter_dimension=1, tiled=True)  61.3 us
    psum x1, waiting for transfers between devices, per_device(): lax.psum(jnp.dot(cross_mix, cross_out_w, preferred_element_type=jnp.float...  50.7 us
  transfers between devices with their start and end apart: 13, of which 10 were waited for; matrix products, arithmetic and copies ran while one was open for 21% of the time, Pallas kernels for 0%

commit v1 on v0

--- a/solution.py
+++ b/solution.py
@@ -7,6 +7,7 @@
 
 HEAD_DIM = 64
 STRETCH = 64
+_start_trees = lambda slab_in: jnp.sum(jax.lax.all_gather(slab_in, axis_name="tp"), axis=0)
 
 
 def norm_forward(field, gain, shift):
@@ -194,9 +195,7 @@
     pre_act = jnp.dot(ln_three, mlp_in_w, preferred_element_type=jnp.float32) + mlp_in_b
     act, gelu_pull = jax.vjp(exact_gelu, pre_act)
     act_low = act.astype(jnp.bfloat16)
-    mlp = (
-        lax.psum(jnp.dot(act_low, mlp_out_w, preferred_element_type=jnp.float32), "tp") + mlp_out_b
-    )
+    mlp = _start_trees(jnp.dot(act_low, mlp_out_w, preferred_element_type=jnp.float32)) + mlp_out_b
     output = lax.dynamic_slice_in_dim(hidden_two + mlp, own_start, own_width, 1).astype(
         jnp.bfloat16
     )

time: 995 us -> 1010 us (1.015)
  local copies, waits for them, and re-layouts: 117 us -> 128 us
  other arithmetic: 57.1 us -> 67.9 us
    psum x1, waiting for transfers between devices: 72.7 us -> 45.6 us  [per_device(): lax.psum(jnp.einsum('tcf,dcf->td', grad_qkv, self_qkv_w, preferred_elemen...]
    all_gather x0 -> x1, waiting for transfers between devices: none -> 10.7 us  [jax.lax.all_gather(slab_in, axis_name='tp')]
    unnamed x226 -> x192, local copies, waits for them, and re-layouts: 23.9 us -> 20.9 us
  transfers between devices with their start and end apart: 13 -> 14, of which waited for: 10 -> 11; matrix products, arithmetic and copies ran while one was open for 21% -> 23% of each run, Pallas kernels for 0% -> 0%
where the time goes in v1:
time: 1010 us; the launch traced here: 1000 us
  waiting for transfers between devices  571 us (57%)
  matrix products  158 us (16%)
  local copies, waits for them, and re-layouts  128 us (13%)
  other arithmetic  67.9 us (7%)
  blocking collectives  61.8 us (6%)
  between operations  16.9 us (2%)
    reduce_scatter x1, waiting for transfers between devices, per_device(): lax.psum_scatter(mlp_out_w_grad, 'dp', scatter_dimension=1, tiled=True)  79.3 us
    reduce_scatter x1, waiting for transfers between devices, per_device(): lax.psum_scatter(mlp_in_w_grad, 'dp', scatter_dimension=0, tiled=True)  78.9 us
    reduce_scatter x1, waiting for transfers between devices, per_device(): lax.psum_scatter(self_qkv_w_grad, 'dp', scatter_dimension=0, tiled=True)  71.6 us
    psum x1, blocking collectives, per_device(): lax.psum((gain_grads, shift_grads, self_qkv_b_grad, self_out_b_grad, cros...  61.8 us
    reduce_scatter x1, waiting for transfers between devices, per_device(): lax.psum_scatter(self_out_w_grad, 'dp', scatter_dimension=1, tiled=True)  61.4 us
    reduce_scatter x1, waiting for transfers between devices, per_device(): lax.psum_scatter(cross_q_w_grad, 'dp', scatter_dimension=0, tiled=True)  61.3 us
    psum x1, waiting for transfers between devices, per_device(): lax.psum(jnp.dot(cross_mix, cross_out_w, preferred_element_type=jnp.float...  51.2 us
    psum x1, waiting for transfers between devices, per_device(): lax.psum(jnp.einsum('tf,df->td', grad_pre, mlp_in_w, preferred_element_ty...  48.9 us
  transfers between devices with their start and end apart: 14, of which 11 were waited for; matrix products, arithmetic and copies ran while one was open for 23% of the time, Pallas kernels for 0%

profile of v1, /device:TPU:0, one launch (start us, length us, event | category | flops | bytes accessed | tf_op | source)
XLA Modules:
  0.0 1004.8 jit_solution(11979706225787758646)
XLA Ops:
  11.8 2.8 convolution_add_fusion.1
  20.6 2.4 subtract_convert_fusion.2
  24.2 2.2 copy.158
  28.2 2.2 copy.159
  30.4 20.7 %while.30 = (s32[]{:T(128)}, bf16[6,512,64]{1,2,0:T(8,128)(2,1)S(1)}, f32[6,512,1]{1,2,0:T(1,128)}, bf16[6,512,64]{2,1,0:T(8,128)(2,1)}, bf16[6,512,64]{2,1,0:T(...) while((s32[]{:T(128)}, ...), condition=%wide.region_6.7_spmd.clone.clone, body=%wide.region_3.6_spmd.clone.sunk.clone | while | flops 70254080 | bytes 3701353 | solution.py:152
  51.1 3.0 fusion.123
  55.0 4.3 add_convert_fusion.1
  59.3 2.8 copy.162
  65.7 4.0 gather_fusion
  69.7 6.0 copy.165
  75.8 5.7 reshape.384
  81.4 3.9 fusion.120
  85.3 23.2 %all-reduce.10.cloned.1.call-done = f32[512,768]{1,0:T(8,128)} async-done(((f32[512,768]{1,0:T(8,128)}), f32[512,768]{1,0:T(8,128)}) %all-reduce.10.cloned.1.call-update) | async-done | bytes 1572880 | tf_op jit(solution)/shard_map/psum | solution.py:157
  114.4 2.3 copy.181
  116.7 2.8 multiply_reduce_fusion.2
  122.1 2.4 convolution_bitcast_fusion.6
  126.6 2.6 reshape.386
  133.7 51.2 %all-reduce.12.cloned.1.call-done = f32[512,768]{1,0:T(8,128)} async-done(((f32[512,768]{1,0:T(8,128)}), f32[512,768]{1,0:T(8,128)}) %all-reduce.12.cloned.1.call-update) | async-done | bytes 1572880 | tf_op jit(solution)/shard_map/psum | solution.py:190
  184.9 2.3 fusion.117
  189.9 10.2 %convert_reduce_fusion = (f32[1536]{0:T(1024)}, bf16[512,1536]{1,0:T(8,128)(2,1)S(1)}, f32[512,1536]{1,0:T(8,128)}) fusion(f32[512,1536]{1,0:T(8,128)S(1)} %convolution_add_fusion, bf16[512,768]{1,0:T(8,128)(2,1)S(1)} %copy-done.15, bf16[1536,768]{1,0:T(8,128)(2,1)S(1)} %copy-done), kind=kOutput, calls=%fused_computation.61 | convolution fusion | flops 1266153984 | bytes 11016192 | tf_op jit(solution)/shard_map/td,fd->tf/dot_general | solution.py:205
  201.3 2.6 fusion.125
  206.6 48.9 %all-reduce.14.cloned.1.call-done = f32[512,768]{1,0:T(8,128)} async-done(((f32[512,768]{1,0:T(8,128)}), f32[512,768]{1,0:T(8,128)}) %all-reduce.14.cloned.1.call-update) | async-done | bytes 1572880 | tf_op jit(solution)/shard_map/psum | solution.py:209
  255.6 3.2 multiply_reduce_fusion.3
  263.5 2.3 concatenate.39
  267.5 3.7 multiply_reduce_fusion.1
  273.7 2.2 multiply_bitcast_fusion
  279.9 3.0 fusion.84
  283.2 3.4 convolution_bitcast_fusion.2
  286.6 3.4 pad_maximum_fusion
  290.0 13.6 %copy.183 = f32[8,256,2,6,64]{4,3,2,1,0:T(8,128)} copy(f32[8,256,2,6,64]{1,4,3,0,2:T(8,128)} %pad_maximum_fusion) | data formatting | bytes 12582912 | tf_op jit(solution)/shard_map/stack | solution.py:260
  303.6 14.9 %reshape.389 = f32[16,98304]{1,0:T(8,128)} reshape(f32[8,256,2,6,64]{4,3,2,1,0:T(8,128)} %copy.183) | data formatting | bytes 12582912 | tf_op jit(solution)/shard_map/reshape | solution.py:260
  318.5 6.3 convolution_convert_fusion
  324.8 3.9 convert_element_type.173
  328.7 4.7 convolution_bitcast_fusion.4
  333.4 5.3 copy.188
  338.8 3.6 multiply_convert_fusion.2
  343.6 2.5 fusion.124
  346.4 3.2 multiply_reduce_fusion.4
  355.4 2.2 copy.174
  357.6 57.2 %while.31 = (s32[]{:T(128)}, f32[6,512,64]{1,2,0:T(8,128)}, f32[6,512,64]{1,2,0:T(8,128)}, bf16[6,512,64]{1,2,0:T(8,128)(2,1)}, bf16[6,512,64]{2,1,0:T(8,128)(2,...) while((s32[]{:T(128)}, f32[6,512,64]{1,2,0:T(8,128)}, ...), condition=%wide.region_25.26_spmd.clone.clone, body=%wide.region_23.25_spmd.clone.sunk.clone | while | flops 171245056 | bytes 12345017 | solution.py:295
  416.7 2.4 subtract_convert_fusion.1
  425.5 4.3 convolution_bitcast_fusion.5
  429.9 4.9 convolution_bitcast_fusion.3
  434.9 3.0 fusion.81
  438.0 3.0 fusion.83
  441.1 3.2 fusion.108
  444.3 6.0 fusion.111
  450.4 5.2 fusion.126
  456.3 4.4 fusion.78
  467.0 4.1 fusion.62
  472.7 10.7 %all-gather.3.cloned.1.call-done = f32[1024,768]{1,0:T(8,128)} async-done(((f32[512,768]{1,0:T(8,128)}), f32[1024,768]{1,0:T(8,128)}) %all-gather.3.cloned.1.call-update) | async-done | bytes 3145744 | tf_op jit(solution)/shard_map/all_gather | solution.py:10
  483.4 3.4 reduce_sum.290
  489.3 2.2 fusion.75
  491.6 45.6 %all-reduce.18.cloned.1.call-done = f32[512,768]{1,0:T(8,128)} async-done(((f32[512,768]{1,0:T(8,128)}), f32[512,768]{1,0:T(8,128)}) %all-reduce.18.cloned.1.call-update) | async-done | bytes 1572880 | tf_op jit(solution)/shard_map/psum | solution.py:307
  537.3 2.1 fusion.59
  539.5 61.8 %all-reduce.2 = (f32[3,768]{1,0:T(4,128)}, f32[3,768]{1,0:T(4,128)}, f32[3,384]{1,0:T(4,128)}, f32[768]{0:T(1024)}, f32[384]{0:T(512)}, /*index=5*/f32[384]{0:T(...) all-reduce(f32[3,768]{1,0:T(4,128)S(1)} %pad_maximum_fusion.12, ...), channel_id=1, replica_groups=mesh['dp'=16,'tp'=2] {'dp'}, use_global_device_ids=true, to_apply=%region_33.34 | all-reduce | flops 10368 | bytes 82944 | tf_op jit(solution)/shard_map/psum | solution.py:343
  601.3 2.2 fusion.114
  604.5 2.4 convert_element_type.169
  606.9 38.5 %reduce-scatter.16.cloned.1.call-done = f32[384,48]{0,1:T(8,128)} async-done(((f32[384,768]{0,1:T(8,128)}), f32[384,48]{0,1:T(8,128)}) %reduce-scatter.16.cloned.1.call-update) | async-done | bytes 73744 | tf_op jit(solution)/shard_map/reduce_scatter | solution.py:327
  645.4 61.3 %reduce-scatter.14.cloned.1.call-done = f32[48,384]{1,0:T(8,128)} async-done(((f32[768,384]{1,0:T(8,128)}), f32[48,384]{1,0:T(8,128)}) %reduce-scatter.14.cloned.1.call-update) | async-done | bytes 73744 | tf_op jit(solution)/shard_map/reduce_scatter | solution.py:325
  706.7 61.4 %reduce-scatter.12.cloned.1.call-done = f32[384,48]{0,1:T(8,128)} async-done(((f32[384,768]{0,1:T(8,128)}), f32[384,48]{0,1:T(8,128)}) %reduce-scatter.12.cloned.1.call-update) | async-done | bytes 73744 | tf_op jit(solution)/shard_map/reduce_scatter | solution.py:324
  768.1 78.9 %reduce-scatter.18.cloned.1.call-done = f32[48,1536]{1,0:T(8,128)} async-done(((f32[768,1536]{1,0:T(8,128)}), f32[48,1536]{1,0:T(8,128)}) %reduce-scatter.18.cloned.1.call-update) | async-done | bytes 294928 | tf_op jit(solution)/shard_map/reduce_scatter | solution.py:328
  847.0 79.3 %reduce-scatter.20.cloned.1.call-done = f32[1536,48]{0,1:T(8,128)} async-done(((f32[1536,768]{0,1:T(8,128)}), f32[1536,48]{0,1:T(8,128)}) %reduce-scatter.20.cloned.1.call-update) | async-done | bytes 294928 | tf_op jit(solution)/shard_map/reduce_scatter | solution.py:329
  926.2 71.6 %reduce-scatter.10.cloned.1.call-done = f32[48,3,384]{2,0,1:T(8,128)} async-done(((f32[768,3,384]{2,0,1:T(8,128)}), f32[48,3,384]{2,0,1:T(8,128)}) %reduce-scatter.10.cloned.1.call-update) | async-done | bytes 221200 | tf_op jit(solution)/shard_map/reduce_scatter | solution.py:323
  (406 shorter events, 156.2 us)
Async XLA Ops:
  7.2 182.7 %copy-start = (bf16[1536,768]{1,0:T(8,128)(2,1)S(1)}, bf16[1536,768]{1,0:T(8,128)(2,1)}, u32[]{:S(2)}) copy-start(bf16[1536,768]{1,0:T(8,128)(2,1)} %param.46) | copy-start | bytes 7077892
  7.2 101.3 %all-reduce.10.cloned.1.call-start = ((), (), s32[]{:S(2)}) async-start(), calls=%async_computation.7 | async-start | bytes 3145728 | tf_op jit(solution)/shard_map/psum | solution.py:157
  8.7 10.3 %copy-start.24 = (bf16[6,512,64]{1,2,0:T(8,128)(2,1)}, bf16[6,512,64]{1,2,0:T(8,128)(2,1)S(1)}, u32[]{:S(2)}) copy-start(bf16[6,512,64]{1,2,0:T(8,128)(2,1)S(1)} %fusion.122) | copy-start | bytes 1179652
  10.2 4.5 copy-start.46
  11.1 3.5 copy-start.54
  18.3 4.7 copy-start.52
  24.2 6.2 copy-start.28
  24.2 6.2 copy-start.77
  51.1 3.8 copy-start.82
  54.1 130.8 %all-reduce.12.cloned.1.call-start = ((), (), s32[]{:S(2)}) async-start(), calls=%async_computation.8 | async-start | bytes 3145728 | tf_op jit(solution)/shard_map/psum | solution.py:190
  81.4 27.1 %copy-start.88 = (f32[768]{0:T(1024)S(1)}, f32[768]{0:T(1024)}, u32[]{:S(2)}) copy-start(f32[768]{0:T(1024)} %param.37) | copy-start | bytes 9220
  119.5 86.5 %copy-start.41 = (f32[8,6,64]{2,1,0:T(8,128)}, f32[8,6,64]{2,1,0:T(8,128)S(1)}, u32[]{:S(2)}) copy-start(f32[8,6,64]{2,1,0:T(8,128)S(1)} %get-tuple-element.441) | copy-start | bytes 36868
  120.6 85.4 %copy-start.43 = (f32[8,6,64]{2,1,0:T(8,128)}, f32[8,6,64]{2,1,0:T(8,128)S(1)}, u32[]{:S(2)}) copy-start(f32[8,6,64]{2,1,0:T(8,128)S(1)} %fusion.50) | copy-start | bytes 36868
  131.2 53.7 %copy-start.81 = (f32[768]{0:T(1024)S(1)}, f32[768]{0:T(1024)}, u32[]{:S(2)}) copy-start(f32[768]{0:T(1024)} %param.43) | copy-start | bytes 9220
  133.2 122.3 %all-reduce.14.cloned.1.call-start = ((), (), s32[]{:S(2)}) async-start(), calls=%async_computation.9 | async-start | bytes 3145728 | tf_op jit(solution)/shard_map/psum | solution.py:209
  184.9 3.4 copy-start.90
  187.5 71.3 %copy-start.57 = (f32[512]{0:T(512)}, f32[512]{0:T(512)S(1)}, u32[]{:S(2)}) copy-start(f32[512]{0:T(512)S(1)} %fusion.101) | copy-start | bytes 6148
  189.9 10.2 %copy-start.30 = (f32[512,1536]{1,0:T(8,128)}, f32[512,1536]{1,0:T(8,128)S(1)}, u32[]{:S(2)}) copy-start(f32[512,1536]{1,0:T(8,128)S(1)} %convolution_add_fusion) | copy-start | bytes 9437188
  203.9 142.5 %all-reduce.16.cloned.1.call-start = ((), (), s32[]{:S(2)}) async-start(), calls=%async_computation.10 | async-start | bytes 3145728 | tf_op jit(solution)/shard_map/psum | solution.py:281
  255.6 3.3 copy-start.6
  255.6 3.3 copy-start.20
  263.5 3.6 copy-start.42
  267.4 3.7 copy-start.29
  267.5 3.7 copy-start.4
  282.9 188.2 %all-reduce.20.cloned.1.call-start = ((), (), s32[]{:S(2)}) async-start(), calls=%async_computation.20 | async-start | bytes 4718592
  283.1 3.4 copy-start.12
  338.8 144.6 %all-gather.3.cloned.1.call-start = ((), (), s32[]{:S(2)}) async-start(), calls=%async_computation.19 | async-start | bytes 4718592 | tf_op jit(solution)/shard_map/all_gather | solution.py:10
  346.1 191.1 %all-reduce.18.cloned.1.call-start = ((), (), s32[]{:S(2)}) async-start(), calls=%async_computation.11 | async-start | bytes 3145728 | tf_op jit(solution)/shard_map/psum | solution.py:307
  346.4 3.9 copy-start.2
  346.4 3.9 copy-start.19
  354.2 3.4 copy-start.78
  354.2 3.4 copy-start.89
  363.3 3.8 copy-start.26
  372.9 3.8 copy-start.26
  382.4 3.8 copy-start.26
  391.9 3.8 copy-start.26
  401.5 3.8 copy-start.26
  411.0 3.8 copy-start.26
  429.8 174.6 %reduce-scatter.8.cloned.1.call-start = ((), (), s32[]{:S(2)}) async-start(), calls=%async_computation.12 | async-start | bytes 4718592 | tf_op jit(solution)/shard_map/reduce_scatter | solution.py:278
  434.9 210.5 %reduce-scatter.16.cloned.1.call-start = ((), (), s32[]{:S(2)}) async-start(), calls=%async_computation.16 | async-start | bytes 1253376 | tf_op jit(solution)/shard_map/reduce_scatter | solution.py:327
  437.9 268.7 %reduce-scatter.14.cloned.1.call-start = ((), (), s32[]{:S(2)}) async-start(), calls=%async_computation.15 | async-start | bytes 1253376 | tf_op jit(solution)/shard_map/reduce_scatter | solution.py:325
  441.0 3.3 copy-start.58
  441.0 3.3 copy-start.87
  441.0 327.1 %reduce-scatter.12.cloned.1.call-start = ((), (), s32[]{:S(2)}) async-start(), calls=%async_computation.14 | async-start | bytes 1253376 | tf_op jit(solution)/shard_map/reduce_scatter | solution.py:324
  444.3 402.7 %reduce-scatter.18.cloned.1.call-start = ((), (), s32[]{:S(2)}) async-start(), calls=%async_computation.17 | async-start | bytes 5013504 | tf_op jit(solution)/shard_map/reduce_scatter | solution.py:328
  450.4 475.9 %reduce-scatter.20.cloned.1.call-start = ((), (), s32[]{:S(2)}) async-start(), calls=%async_computation.18 | async-start | bytes 5013504 | tf_op jit(solution)/shard_map/reduce_scatter | solution.py:329
  455.7 542.2 %reduce-scatter.10.cloned.1.call-start = ((), (), s32[]{:S(2)}) async-start(), calls=%async_computation.13 | async-start | bytes 3760128 | tf_op jit(solution)/shard_map/reduce_scatter | solution.py:323
  460.8 3.3 copy-start.65
  460.8 3.9 copy-start.64
  483.4 3.5 copy-start.67
  483.4 4.0 copy-start.66
  483.4 4.6 copy-start.35
  489.3 47.9 %copy-start.56 = (f32[512]{0:T(512)S(1)}, f32[512]{0:T(512)}, u32[]{:S(2)}) copy-start(f32[512]{0:T(512)} %copy-done.54) | copy-start | bytes 6148
  491.5 47.8 %copy-start.69 = (f32[1,768]{1,0:T(1,128)S(1)}, f32[1,768]{1,0:T(1,128)}, u32[]{:S(2)}) copy-start(f32[1,768]{1,0:T(1,128)} %reshape.392) | copy-start | bytes 9220
  491.5 47.8 %copy-start.71 = (f32[1,768]{1,0:T(1,128)S(1)}, f32[1,768]{1,0:T(1,128)}, u32[]{:S(2)}) copy-start(f32[1,768]{1,0:T(1,128)} %reshape.391) | copy-start | bytes 9220
  491.5 47.9 %copy-start.68 = (f32[1,768]{1,0:T(1,128)S(1)}, f32[1,768]{1,0:T(1,128)}, u32[]{:S(2)}) copy-start(f32[1,768]{1,0:T(1,128)} %reshape.395) | copy-start | bytes 9220
  491.6 47.9 %copy-start.70 = (f32[1,768]{1,0:T(1,128)S(1)}, f32[1,768]{1,0:T(1,128)}, u32[]{:S(2)}) copy-start(f32[1,768]{1,0:T(1,128)} %reshape.394) | copy-start | bytes 9220
  491.6 47.9 %copy-start.61 = (f32[768]{0:T(1024)S(1)}, f32[768]{0:T(1024)}, u32[]{:S(2)}) copy-start(f32[768]{0:T(1024)} %get-tuple-element.399) | copy-start | bytes 9220
  491.6 47.9 %copy-start.62 = (f32[768]{0:T(1024)S(1)}, f32[768]{0:T(1024)}, u32[]{:S(2)}) copy-start(f32[768]{0:T(1024)} %get-tuple-element.401) | copy-start | bytes 9220
  491.6 47.9 %copy-start.63 = (f32[768]{0:T(1024)S(1)}, f32[768]{0:T(1024)}, u32[]{:S(2)}) copy-start(f32[768]{0:T(1024)} %get-tuple-element.429) | copy-start | bytes 9220
  491.6 47.9 %copy-start.72 = (f32[384]{0:T(512)S(1)}, f32[384]{0:T(512)}, u32[]{:S(2)}) copy-start(f32[384]{0:T(512)} %convert_reduce_fusion.6) | copy-start | bytes 4612
  491.6 47.9 %copy-start.73 = (f32[384]{0:T(512)S(1)}, f32[384]{0:T(512)}, u32[]{:S(2)}) copy-start(f32[384]{0:T(512)} %fusion.62) | copy-start | bytes 4612
  491.6 47.9 %copy-start.75 = (f32[1536]{0:T(1024)S(1)}, f32[1536]{0:T(1024)}, u32[]{:S(2)}) copy-start(f32[1536]{0:T(1024)} %get-tuple-element.396) | copy-start | bytes 18436
  491.6 109.7 %copy-start.50 = (f32[512]{0:T(512)S(1)}, f32[512]{0:T(512)}, u32[]{:S(2)}) copy-start(f32[512]{0:T(512)} %copy-done.49) | copy-start | bytes 6148
  (55 other events, 81.5 us)
Sparse Core Ops, SparseCore 0:
  54.2 54.2 all-reduce.9
  133.3 51.5 all-reduce.11
  204.0 51.5 all-reduce.13
  283.0 51.5 all-reduce.15
  338.9 99.5 all-reduce.19
  439.9 43.4 all-gather.2
  485.7 51.5 all-reduce.17
  539.5 43.4 reduce-scatter.7
  587.2 58.1 reduce-scatter.15
  649.4 57.1 reduce-scatter.13
  710.9 57.1 reduce-scatter.11
  772.4 74.5 reduce-scatter.17
  851.4 74.7 reduce-scatter.19
  930.5 67.2 reduce-scatter.9
